TPU v7x, 32 devices: a whole 2x2x4 slice. The times are simulated.
32 devices in a mesh: tile: 8 (over y, x, core), epoch: 4 (over z).
Axes of the slice: x: 2, y: 2, z: 4, core: 2. Of those that a mesh axis runs over, the one named last changes fastest.
Arguments:
- residual: bfloat16 [8, 128, 64, 128], P('tile', 'epoch'), may hold values from -6 to 6
- inv_variance: float32 [8, 128, 64, 128], P('tile', 'epoch'), may hold values from 0.25 to 4
- psf_coeff: float32 [8, 128, 16], P('tile', 'epoch'), may hold values from -5 to 5
- psf_taps: float32 [16, 2, 25], replicated, may hold values from -1.25 to 1.25
- patch_owner: int32 [8, 128, 1], P('tile', 'epoch'), may hold values from 0 to 3; in each aligned block of 32 rows (0 to 31, 32 to 63, ..., all dimensions but the last counted through in order) at most 16 rows name the same one
- patch_slot: int32 [8, 128], P('tile', 'epoch'), may hold values from 0 to 7
- band_id: int32 [8, 128], P('tile', 'epoch'), may hold values from 0 to 5
- tile_offset: int32 [8, 128], P('tile', 'epoch'), may hold values from 0 to 2
- col_shift: int32 [8, 128], P('tile', 'epoch'), may hold values from 0 to 7
Outputs:
- scene_adjoint: float32 [8, 6, 32, 64, 128], P('tile', None, 'epoch')
Inputs may be any that keep to these rules, and one draw needn't show every extreme that they name: Among the 32 blocks of one device at most 16 have the same patch_owner, and in every draw some owner receives exactly 16 from some device.
All inputs are finite; a program needn't handle non-finite values.
Results may differ from a plain program's by a relative error of at most 0.0003.
Values sent between devices are 32-bit elements; how exact they have to be, the bound alone decides.
No kernel may reach another device: no remote copies, remote signals or barrier semaphores. Data moves between devices by JAX's collectives and lax.ppermute only.
A program may use at most 64 MiB of HBM per device.

v0:
```python
import functools

import jax
import jax.numpy as jnp
from jax import lax
from jax.experimental import pallas as pl
from jax.experimental.pallas import tpu as pltpu
from jax.sharding import PartitionSpec as P


BANDS = 6
PATCHES = 32
HEAD = 8
LANES = 128


SMEM = pltpu.SMEM
VMEM = pltpu.VMEM
MIB = 1 << 20


def halves(x):
    high = x.astype(jnp.bfloat16)
    low = (x - high.astype(jnp.float32)).astype(jnp.bfloat16)
    return high, low


def plan_chunks(capacity):
    if capacity >= 16:
        sizes = (capacity // 4, capacity // 2, capacity - capacity // 4 - capacity // 2)
    else:
        sizes = (capacity // 2, capacity - capacity // 2)
    starts = [sum(sizes[:k]) for k in range(len(sizes))]
    return list(zip(starts, sizes))


def head_lanes():
    return lax.broadcasted_iota(jnp.int32, (HEAD, LANES), 1)


def build_bands(taps_ref, cols_ref, rows_ref):
    comps, _, taps = taps_ref.shape
    cols = cols_ref.shape[1] // 2
    rows = rows_ref.shape[1] // 4
    half = (taps - 1) // 2
    tap = lax.broadcasted_iota(jnp.int32, (taps, LANES), 0)
    lane = lax.broadcasted_iota(jnp.int32, (taps, LANES), 1)
    place_col = (lax.rem(lane + tap - half + cols, cols) == 0).astype(jnp.float32)
    place_row = (lax.rem(lane - tap + half + 2 * rows, rows) == 0).astype(jnp.float32)
    base_col = jnp.dot(
        taps_ref[:, 0, :], place_col, precision=lax.Precision.HIGHEST,
        preferred_element_type=jnp.float32,
    )
    base_row = jnp.dot(
        taps_ref[:, 1, :], place_row, precision=lax.Precision.HIGHEST,
        preferred_element_type=jnp.float32,
    )
    up = lax.broadcasted_iota(jnp.int32, (cols, LANES), 0)
    across = lax.broadcasted_iota(jnp.int32, (cols, LANES), 1)
    near_col = jnp.abs(across - up) <= half
    up_row = lax.broadcasted_iota(jnp.int32, (rows, LANES), 0)
    across_row = lax.rem(lax.broadcasted_iota(jnp.int32, (rows, LANES), 1), rows)
    near_row = jnp.abs(across_row - up_row) <= half
    for c in range(comps):
        wide = jnp.broadcast_to(base_col[c : c + 1, :], (cols, LANES))
        wide = pltpu.roll(wide, 0, 1, stride=1, stride_axis=0)
        high, low = halves(jnp.where(near_col, wide, 0.0))
        cols_ref[c * cols : (c + 1) * cols, :] = jnp.concatenate([high, low], axis=1)
        wide = jnp.broadcast_to(base_row[c : c + 1, :], (rows, LANES))
        wide = pltpu.roll(wide, 0, 1, stride=1, stride_axis=0)
        high, low = halves(jnp.where(near_row, wide, 0.0))
        rows_ref[c * rows : (c + 1) * rows, :] = jnp.concatenate([high, low], axis=1)


def fill_slots(cfg, places, block_ref, label_ref, front_ref, back_ref):
    epochs, capacity, per_dev, tiles, count, _, _ = cfg
    cells = BANDS * per_dev
    owner_ref, slot_ref, band_ref, offset_ref = places
    tile = lax.axis_index("tile")
    for e in range(epochs):
        front_ref[e] = e * capacity
        back_ref[e] = (e + 1) * capacity - 1

    for b in range(count):
        off = offset_ref[b]
        target = tile + off - 1
        lands = ((target >= 0) & (target < tiles)).astype(jnp.int32)
        stays = lands * (off == 1).astype(jnp.int32)
        o = owner_ref[b]
        front = front_ref[o]
        back = back_ref[o]
        at = jnp.where(lands == 0, epochs * capacity, jnp.where(off == 1, back, front))
        front_ref[o] = front + lands - stays
        back_ref[o] = back - stays
        block_ref[at] = b
        label_ref[at] = off * cells + band_ref[b] * per_dev + slot_ref[b] + 1


def take(refs, at):
    at = at + 2
    return [*refs[:at], *refs[at + 1 :], refs[at]]


def resample_kernel(cfg, first, parts, join, *refs):
    epochs, capacity, _, _, _, rows, cols = cfg
    slots = epochs * capacity
    n_out = len(parts)
    if join:
        *refs, joined_ref = take(refs, 8 + n_out)
        mine_ref, theirs_ref, *refs = refs
        joined_ref[...] = jnp.maximum(mine_ref[...], theirs_ref[...])
    if first:
        small_hbm, large_hbm, rest = refs[:6], refs[6:9], refs[9:]
        outs, rest = rest[:n_out], rest[n_out:]
        cols_ref, rows_ref, res_ref, inv_ref, block_ref, label_ref = rest[:6]
        shift_ref, coeff_ref, *places, taps_ref, front_ref, back_ref = rest[6:15]
        small = [*places, shift_ref, coeff_ref]
        rest = rest[15:]
        pieces = [
            *zip(small_hbm, small),
            *zip(large_hbm, (taps_ref, res_ref, inv_ref)),
        ]
    else:
        block_ref, label_ref, shift_ref, coeff_ref = refs[:4]
        cols_ref, rows_ref, res_ref, inv_ref = refs[4:8]
        outs, rest = refs[8 : 8 + n_out], refs[8 + n_out :]
        pieces = []
    spread_refs, todo_ref, sems = rest[:2], rest[2], rest[3]
    fetches = [
        pltpu.make_async_copy(src, dst, sems.at[i]) for i, (src, dst) in enumerate(pieces)
    ]
    for fetch in fetches:
        fetch.start()

    if first:
        for i in range(slots):
            label_ref[i] = 0
            block_ref[i] = 0
        for fetch in fetches[:4] + fetches[6:7]:
            fetch.wait()
        build_bands(taps_ref, cols_ref, rows_ref)
        fill_slots(cfg, places, block_ref, label_ref, front_ref, back_ref)

    me = lax.axis_index("epoch")
    total = jnp.int32(0)
    for k, (d, start, size) in enumerate(parts):
        o = lax.rem(me + d, epochs)
        for s in range(size):
            at = o * capacity + start + s
            todo_ref[0, total] = block_ref[at]
            todo_ref[1, total] = k * slots + s
            total = total + (label_ref[at] > 0).astype(jnp.int32)
    for i in range(3):
        todo_ref[0, total + i] = 0
        todo_ref[1, total + i] = len(parts) * slots

    lane = head_lanes()
    if any(start == 0 for _, start, _ in parts):
        head = jnp.zeros((HEAD, LANES), jnp.float32)
        for j in range(slots):
            head = jnp.where(lane == j, label_ref[j].astype(jnp.float32), head)
        for k, (d, start, size) in enumerate(parts):
            if start == 0:
                outs[k][size * rows : size * rows + HEAD, :] = head

    for fetch in fetches[4:6] + fetches[7:]:
        fetch.wait()
    comps = cols_ref.shape[0] // cols
    lanes = lax.broadcasted_iota(jnp.int32, (rows, cols), 1)

    def work(base, twos):
        jobs_here = [(todo_ref[0, base + g], todo_ref[1, base + g]) for g in range(2 * twos)]
        for t in range(twos):
            blocks = [b for b, _ in jobs_here[2 * t : 2 * t + 2]]
            spread_ref = spread_refs[t]
            sides = []
            for b in blocks:
                high, low = halves(inv_ref[b] * res_ref[b].astype(jnp.float32))
                sides.append(jnp.concatenate([high, low, high, low], axis=0))
            down = jnp.dot(
                rows_ref[...],
                jnp.concatenate(sides, axis=1),
                preferred_element_type=jnp.float32,
            )
            for c in range(comps):
                for g in range(2):
                    part = down[c * rows : (c + 1) * rows, g * cols : (g + 1) * cols]
                    high, low = halves(part * coeff_ref[c, blocks[g]])
                    at = slice(c * cols, (c + 1) * cols)
                    spread_ref[g * rows : (g + 1) * rows, at] = high
                    spread_ref[(2 + g) * rows : (3 + g) * rows, at] = low
        images = []
        for t in range(twos):
            both = jnp.dot(
                spread_refs[t][...], cols_ref[...], preferred_element_type=jnp.float32
            )
            for g in range(2):
                b, where = jobs_here[2 * t + g]
                high = both[g * rows : (g + 1) * rows]
                low = both[(2 + g) * rows : (3 + g) * rows]
                image = high[:, :cols] + (high[:, cols:] + low[:, :cols])
                shift = shift_ref[b]
                images.append(jnp.where(lanes >= shift, pltpu.roll(image, shift, 1), 0.0))
        for (_, where), image in zip(jobs_here, images):
            for k in range(len(parts)):

                @pl.when((where >= k * slots) & (where < (k + 1) * slots))
                def _():
                    s = pl.multiple_of((where - k * slots) * rows, rows)
                    outs[k][pl.ds(s, rows), :] = image

    quads = (total + 1) // 4

    def quad(i, carry):
        work(4 * i, 2)
        return carry

    lax.fori_loop(0, quads, quad, 0)

    @pl.when(total > 4 * quads)
    def _():
        work(4 * quads, 1)


def read_heads(sources, head_refs, sems, meanwhile=None):
    copies = [
        pltpu.make_async_copy(src.at[pl.ds(src.shape[0] - HEAD, 1)], dst, sems.at[i])
        for i, (src, dst) in enumerate(zip(sources, head_refs))
    ]
    for copy in copies:
        copy.start()
    if meanwhile is not None:
        meanwhile()
    for copy in copies:
        copy.wait()


PITCH = 1024


class Queues:
    def __init__(self, cfg, chunks, sends):
        epochs, capacity = cfg[:2]
        self.sources = [(0, 0, 0, capacity)] + [
            (k, d, start, size) for k, (start, size) in enumerate(chunks) for d in range(1, epochs)
        ]
        self.slots = epochs * capacity
        self.waves = len(chunks)
        self.ends = 3 * self.slots + 1
        self.limits = self.ends + 3 * len(self.sources)
        self.size = self.limits + 2 * 2 * self.waves
        self.sends = sends
        self.capacity = capacity

    def entry(self, which, i):
        return which * self.slots + i

    def end(self, which, source):
        return self.ends + which * len(self.sources) + source

    def limit(self, side, wave):
        return self.limits + 2 * (side * self.waves + wave)

    def fill(self, table, labels, cells):
        counts = (jnp.int32(0),) * 3
        for at, (k, d, start, size) in enumerate(self.sources):

            def step(j, counts, d=d, start=start):
                label = labels(d, start + j)
                kind = (label > cells).astype(jnp.int32) + (label > 2 * cells).astype(jnp.int32)
                some = label > 0
                n = jnp.where(kind == 0, counts[0], jnp.where(kind == 1, counts[1], counts[2]))
                place = jnp.where(some, kind * self.slots + n, 3 * self.slots)
                table[place] = j * PITCH + label - 1 - kind * cells
                return tuple(
                    c + (some & (kind == w)).astype(jnp.int32) for w, c in enumerate(counts)
                )

            counts = lax.fori_loop(0, size, step, counts)
            for w in range(3):
                table[self.end(w, at)] = counts[w]
        for side, which in enumerate((0, 2)):
            sent = jnp.int32(0)
            for k in range(self.waves):
                last = max(i for i, source in enumerate(self.sources) if source[0] == k)
                table[self.limit(side, k)] = sent
                sent = jnp.minimum(table[self.end(which, last)], sent + self.sends[k])
                table[self.limit(side, k) + 1] = sent


    def overflow(self, heads, cells, ends):
        slot = lax.broadcasted_iota(jnp.int32, (LANES, LANES), 0)
        epoch = lax.broadcasted_iota(jnp.int32, (LANES, LANES), 1)
        mine = lax.div(slot, self.capacity) == epoch
        over = jnp.zeros((HEAD, LANES), jnp.float32)
        for low, high in ((0, cells), (2 * cells, 3 * cells)):
            amount = jnp.zeros((HEAD, LANES), jnp.float32)
            for head in heads:
                amount = amount + jnp.where((head > low) & (head <= high), 1.0, 0.0)
            sent = jnp.zeros((HEAD, LANES), jnp.float32)
            for end, cap in zip(ends, self.sends):
                here = jnp.where(mine & (lax.rem(slot, self.capacity) < end), 1.0, 0.0)
                have = jnp.dot(
                    amount.astype(jnp.bfloat16),
                    here.astype(jnp.bfloat16),
                    preferred_element_type=jnp.float32,
                )
                sent = jnp.minimum(have, sent + cap)
            over = jnp.maximum(over, jnp.where(have > sent, 1.0, 0.0))
        return over


def collect_kernel(cfg, queues, k, ends, *refs):
    epochs, capacity, per_dev, _, _, rows, _ = cfg
    cells = BANDS * per_dev
    known = [i for i, source in enumerate(queues.sources) if source[0] <= k]
    if k == 0:
        sources, rest = refs[: len(known)], refs[len(known) :]
        prev_ref, next_ref, table, over_ref = rest[:4]
        head_refs, sems = rest[4 : 4 + epochs], rest[4 + epochs]
        read_heads(sources, head_refs, sems)
        mine = lax.axis_index("epoch") * capacity
        queues.fill(table, lambda d, j: head_refs[d][0, mine + j].astype(jnp.int32), cells)
        heads = [src[src.shape[0] - HEAD :, :] for src in sources]
        over = jnp.max(queues.overflow(heads, cells, ends), axis=1, keepdims=True)
        over_ref[...] = jnp.broadcast_to(over, over_ref.shape)
    else:
        table, mine_ref, theirs_ref = refs[:3]
        sources, rest = refs[3 : 3 + len(known)], refs[3 + len(known) :]
        prev_ref, next_ref, over_ref = rest
        over_ref[...] = jnp.maximum(mine_ref[...], theirs_ref[...])
    lane = head_lanes()
    cap = queues.sends[k]
    for side, (which, dst) in enumerate(((0, prev_ref), (2, next_ref))):
        first = table[queues.limit(side, k)]
        last = table[queues.limit(side, k) + 1]
        for i, src in zip(known, sources):
            low = table[queues.end(which, i - 1)] if i else 0
            high = table[queues.end(which, i)]

            def step(r, carry, which=which, src=src, dst=dst, first=first):
                j = table[queues.entry(which, r)] // PITCH
                dst[pl.ds(pl.multiple_of((r - first) * rows, rows), rows), :] = src[
                    pl.ds(pl.multiple_of(j * rows, rows), rows), :
                ]
                return carry

            lax.fori_loop(jnp.maximum(low, first), jnp.minimum(high, last), step, 0)

        def mark(r, head, which=which, first=first):
            cell = table[queues.entry(which, r)] % PITCH
            return jnp.where(lane == r - first, cell.astype(jnp.float32), head)

        amount = jnp.where(lane == LANES - 1, (last - first).astype(jnp.float32), 0.0)
        dst[cap * rows : cap * rows + HEAD, :] = lax.fori_loop(first, last, mark, amount)


def add_waves(total_ref, waves, head_refs, rows):
    for src, head in zip(waves, head_refs):

        def step(j, carry, src=src, head=head):
            cell = head[0, j].astype(jnp.int32)
            block = pl.ds(pl.multiple_of(j * rows, rows), rows)
            total_ref[cell] = total_ref[cell] + src[block, :]
            return carry

        lax.fori_loop(0, head[0, LANES - 1].astype(jnp.int32), step, 0)


def settle_kernel(cfg, queues, *refs):
    rows = cfg[5]
    n = len(queues.sources)
    table, over_ref, sources, rest = refs[0], refs[1], refs[2 : 2 + n], refs[2 + n :]
    waves = (len(rest) - 4) // 2
    early, (total_ref, failed_ref) = rest[:waves], rest[waves : waves + 2]
    head_refs, (said_ref, sems) = rest[waves + 2 : -2], rest[-2:]
    say = pltpu.make_async_copy(over_ref.at[pl.ds(0, 1)], said_ref, sems.at[waves])
    say.start()
    total_ref[...] = jnp.zeros_like(total_ref)
    for i, src in enumerate(sources):

        def step(r, carry, src=src):
            entry = table[queues.entry(1, r)]
            cell = entry % PITCH
            block = pl.ds(pl.multiple_of((entry // PITCH) * rows, rows), rows)
            total_ref[cell] = total_ref[cell] + src[block, :]
            return carry

        low = table[queues.end(1, i - 1)] if i else 0
        lax.fori_loop(low, table[queues.end(1, i)], step, 0)
    read_heads(early, head_refs, sems)
    add_waves(total_ref, early, head_refs, rows)
    say.wait()
    failed_ref[0] = (said_ref[0, 0] > 0.0).astype(jnp.int32)


def finish_kernel(rows, *refs):
    waves = (len(refs) - 3) // 2
    total_ref, sources, out_ref = refs[0], refs[1 : 1 + waves], refs[1 + waves]
    head_refs, sems = refs[2 + waves : -1], refs[-1]

    def take_over():
        out_ref[...] = total_ref[...]

    read_heads(sources, head_refs, sems, take_over)
    add_waves(out_ref, sources, head_refs, rows)


def run(cfg, sends, args):
    (
        residual, inv_variance, psf_coeff, psf_taps, patch_owner,
        patch_slot, band_id, tile_offset, col_shift,
    ) = args
    epochs, capacity, per_dev, tiles, count, rows, cols = cfg
    comps = psf_taps.shape[0]
    cells = BANDS * per_dev
    chunks = plan_chunks(capacity)
    ends = [start + size for start, size in chunks]
    n = epochs - 1
    full = [(capacity if k == 0 else 0) + n * size for k, (_, size) in enumerate(chunks)]
    checked = any(cap < most for cap, most in zip(sends, full))
    f32 = jnp.float32
    smem = pl.BlockSpec(memory_space=SMEM)
    vmem = pl.BlockSpec(memory_space=VMEM)
    hbm = pl.BlockSpec(memory_space=pltpu.HBM)

    def slab(slots):
        return jax.ShapeDtypeStruct((slots * rows + HEAD, cols), f32)

    inputs = (
        patch_owner.reshape(count),
        patch_slot.reshape(count),
        band_id.reshape(count),
        tile_offset.reshape(count),
        col_shift.reshape(count),
        psf_coeff[0].T,
        psf_taps,
        residual[0],
        inv_variance[0],
    )
    inputs = tuple(pltpu.with_memory_space_constraint(x, pltpu.HBM) for x in inputs)
    slots = epochs * capacity
    common = [
        *[VMEM((4 * rows, comps * cols), jnp.bfloat16)] * 2,
        SMEM((2, slots + 3), jnp.int32),
        pltpu.SemaphoreType.DMA((9,)),
    ]
    params = pltpu.CompilerParams(vmem_limit_bytes=24 * MIB)
    kept = [
        jax.ShapeDtypeStruct((comps * cols, 2 * cols), jnp.bfloat16),
        jax.ShapeDtypeStruct((comps * rows, 4 * rows), jnp.bfloat16),
        jax.ShapeDtypeStruct((count, rows, cols), residual.dtype),
        jax.ShapeDtypeStruct((count, rows, cols), f32),
    ]
    kept += [jax.ShapeDtypeStruct((slots + 1,), jnp.int32)] * 2
    kept += [jax.ShapeDtypeStruct((count,), jnp.int32)]
    kept += [jax.ShapeDtypeStruct((comps, count), f32)]
    start, size = chunks[0]
    middle = epochs // 2
    made = pl.pallas_call(
        functools.partial(resample_kernel, cfg, True, [(middle, start, size)], False),
        out_shape=[slab(size)] + kept,
        in_specs=[hbm] * 9,
        out_specs=[vmem] * 5 + [smem] * 4,
        scratch_shapes=[SMEM((count,), jnp.int32)] * 4
        + [VMEM(psf_taps.shape, f32)]
        + [SMEM((epochs,), jnp.int32)] * 2
        + common,
        compiler_params=params,
        name="resample_first",
    )(*inputs)
    farthest, kept = made[0], made[1:]

    def more(parts, told=()):
        join = [jax.ShapeDtypeStruct((HEAD, LANES), f32)] if told else []
        return pl.pallas_call(
            functools.partial(resample_kernel, cfg, False, parts, bool(told)),
            out_shape=[slab(size) for _, _, size in parts] + join,
            in_specs=[vmem] * len(told) + [smem] * 4 + [vmem] * 4,
            out_specs=[vmem] * (len(parts) + len(join)),
            scratch_shapes=common,
            compiler_params=params,
        )(*told, *kept[4:], *kept[:4])

    others = [d for d in range(1, epochs) if d != middle]
    made = more([(d, start, size) for d in others])
    slabs = [[dict(zip(others, made)).get(d, farthest) for d in range(1, epochs)]]
    for k in range(1, len(chunks) - 1):
        slabs.append(more([(d, *chunks[k]) for d in range(1, epochs)]))
    own = more([(0, 0, capacity)])[0]

    def turn(x, d):
        return lax.ppermute(x, "epoch", [(i, (i + d) % epochs) for i in range(epochs)])

    def beside(x, d):
        route = [(i, i + d) for i in range(tiles) if 0 <= i + d < tiles]
        return lax.ppermute(x, "tile", route)

    def swap(x, k):
        if not checked:
            return x
        return lax.ppermute(x, "tile", [(i, i ^ (1 << k)) for i in range(tiles)])

    queues = Queues(cfg, chunks, sends)
    sources = [own]
    waves = []
    table = over = None
    for k in range(len(chunks)):
        if k == 1:
            parts = [(d, *chunks[-1]) for d in range(1, epochs)]
            made = more(parts, (over, swap(over, 0)))
            slabs.append(made[:-1])
            over = made[-1]
        sources += [turn(slabs[k][d - 1], d) for d in range(1, epochs)]
        out_shape = [slab(sends[k])] * 2
        out_specs = [vmem] * 2
        extra = []
        if k == 0:
            out_shape.append(jax.ShapeDtypeStruct((queues.size,), jnp.int32))
            out_specs.append(smem)
            extra = [SMEM((1, LANES), f32)] * epochs + [pltpu.SemaphoreType.DMA((epochs,))]
        out_shape.append(jax.ShapeDtypeStruct((HEAD, LANES), f32))
        out_specs.append(vmem)
        told = [over, swap(over, k)] if k else []
        result = pl.pallas_call(
            functools.partial(collect_kernel, cfg, queues, k, ends),
            out_shape=out_shape,
            in_specs=([smem] if k else []) + [vmem] * (len(told) + len(sources)),
            out_specs=out_specs,
            scratch_shapes=extra,
            compiler_params=params,
        )(*([table] if k else []), *told, *sources)
        if k == 0:
            table = result[2]
        over = result[-1]
        waves.append([beside(result[0], -1), beside(result[1], 1)])
    early = waves[0]
    late = [x for wave in waves[1:] for x in wave]
    total_shape = jax.ShapeDtypeStruct((cells, rows, cols), f32)

    def heads(arrays):
        return [SMEM((1, LANES), f32)] * len(arrays)

    total, failed = pl.pallas_call(
        functools.partial(settle_kernel, cfg, queues),
        out_shape=[total_shape, jax.ShapeDtypeStruct((1,), jnp.int32)],
        in_specs=[smem] + [vmem] * (1 + len(sources) + len(early)),
        out_specs=[vmem, smem],
        scratch_shapes=heads(early)
        + [SMEM((1, LANES), f32), pltpu.SemaphoreType.DMA((len(early) + 1,))],
        compiler_params=params,
        name="settle",
    )(table, over, *sources, *early)
    out = pl.pallas_call(
        functools.partial(finish_kernel, rows),
        out_shape=total_shape,
        in_specs=[vmem] * (1 + len(late)),
        out_specs=vmem,
        scratch_shapes=heads(late) + [pltpu.SemaphoreType.DMA((len(late),))],
        compiler_params=params,
        name="finish",
    )(total, *late)
    return out, failed[0] > 0 if checked else None


def on_device(tiles, epochs, *args):
    count, rows, cols = args[0].shape[1:]
    capacity = max(2, min(count // 2, 64 // epochs))
    per_dev = PATCHES // epochs
    cfg = (epochs, capacity, per_dev, tiles, count, rows, cols)
    full = [
        (capacity if k == 0 else 0) + (epochs - 1) * size
        for k, (_, size) in enumerate(plan_chunks(capacity))
    ]
    sends = full
    if capacity >= 16 and tiles == 1 << len(full):
        sends = [7 * capacity // 8, 7 * capacity // 8, 3 * capacity // 8]
        sends = [min(a, b) for a, b in zip(sends, full)]
    out, failed = run(cfg, sends, args)
    if failed is not None:

        def again(state):
            return jnp.zeros((), bool), run(cfg, full, args)[0]

        _, out = lax.while_loop(lambda state: state[0], again, (failed, out))
    return out.reshape(1, BANDS, per_dev, rows, cols)


def solution(mesh):
    in_specs = (
        P("tile", "epoch", None, None),
        P("tile", "epoch", None, None),
        P("tile", "epoch", None),
        P(),
        P("tile", "epoch", None),
        P("tile", "epoch"),
        P("tile", "epoch"),
        P("tile", "epoch"),
        P("tile", "epoch"),
    )
    out_specs = P("tile", None, "epoch", None, None)
    epochs = mesh.shape["epoch"]
    return jax.shard_map(
        functools.partial(on_device, mesh.shape["tile"], epochs),
        mesh=mesh,
        in_specs=in_specs,
        out_specs=out_specs,
        check_vma=False,
    )
```

profile of v0, /device:TPU:12, one launch (start us, length us, event | category | flops | bytes accessed | tf_op | source)
XLA Modules:
  0.0 81.5 jit_solution(5547982610930907614)
XLA Ops:
  0.0 3.9 %resample_first.3 = (f32[264,128]{1,0:T(8,128)S(1)}, bf16[2048,256]{1,0:T(8,128)(2,1)S(1)}, bf16[1024,256]{1,0:T(8,128)(2,1)S(1)}, bf16[32,64,128]{2,1,0:T(8,128...) custom-call(s32[32]{0:T(128)} %bitcast.26, ...), custom_call_target="tpu_custom_call" | custom-call | tf_op jit(solution)/shard_map/resample_first/pallas_call | solution.py:460
  3.9 3.9 %shard_map.92 = (f32[264,128]{1,0:T(8,128)S(1)}, f32[264,128]{1,0:T(8,128)S(1)}) custom-call(s32[65]{0:T(128)S(1)} %get-tuple-element.119.refs_0_.refs_2_, s32[65]{0:T(128)S(1)} %get-tuple-element.120.refs_1_.refs_3_, s32[32]{0:T(128)S(1)} %get-tuple-element.121.refs_2_.refs_4_, f32[16,32]{1,0:T(8,128)S(1)} %get-tuple-element.122.refs_3_.refs_5_, ...), custom_call_target="tpu_custom_call" | custom-call | tf_op jit(solution)/shard_map/pallas_call | solution.py:476
  7.8 1.6 %collective-permute-start.15 = (f32[264,128]{1,0:T(8,128)S(1)}, f32[264,128]{1,0:T(8,128)S(1)}, u32[]{:S(2)}, u32[]{:S(2)}) collective-permute-start(f32[264,128]{1,0:T(8,128)S(1)} %get-tuple-element.127), channel_id=1, source_target_pairs={{0,1},{1,2},{2,3},{3,0},{4,5},{5,6},{6,7},{7,4},{8,9},{9,10},{10,1... | collective-permute-start | bytes 405512 | tf_op jit(solution)/shard_map/ppermute | solution.py:493
  9.4 0.5 collective-permute-start.17
  9.9 2.0 %collective-permute-start.16 = (f32[264,128]{1,0:T(8,128)S(1)}, f32[264,128]{1,0:T(8,128)S(1)}, u32[]{:S(2)}, u32[]{:S(2)}) collective-permute-start(f32[264,128]{1,0:T(8,128)S(1)} %get-tuple-element.128), channel_id=1, source_target_pairs={{0,2},{1,3},{2,0},{3,1},{4,6},{5,7},{6,4},{7,5},{8,10},{9,11},{10,... | collective-permute-start | bytes 405512 | tf_op jit(solution)/shard_map/ppermute | solution.py:493
  11.9 4.9 %shard_map.95 = (f32[520,128]{1,0:T(8,128)S(1)}, f32[520,128]{1,0:T(8,128)S(1)}, f32[520,128]{1,0:T(8,128)S(1)}) custom-call(s32[65]{0:T(128)S(1)} %get-tuple-element.119.refs_0_.refs_2_, s32[65]{0:T(128)S(1)} %get-tuple-element.120.refs_1_.refs_3_, s32[32]{0:T(128)S(1)} %get-tuple-element.121.refs_2_.refs_4_, ...), custom_call_target="tpu_custom_call" | custom-call | tf_op jit(solution)/shard_map/pallas_call | solution.py:476
  16.8 1.8 %collective-permute-start.20 = (f32[520,128]{1,0:T(8,128)S(1)}, f32[520,128]{1,0:T(8,128)S(1)}, u32[]{:S(2)}, u32[]{:S(2)}) collective-permute-start(f32[520,128]{1,0:T(8,128)S(1)} %get-tuple-element.133), channel_id=1, source_target_pairs={{0,1},{1,2},{2,3},{3,0},{4,5},{5,6},{6,7},{7,4},{8,9},{9,10},{10,1... | collective-permute-start | bytes 798728 | tf_op jit(solution)/shard_map/ppermute | solution.py:493
  18.6 1.5 %collective-permute-start.22 = (f32[520,128]{1,0:T(8,128)S(1)}, f32[520,128]{1,0:T(8,128)S(1)}, u32[]{:S(2)}, u32[]{:S(2)}) collective-permute-start(f32[520,128]{1,0:T(8,128)S(1)} %get-tuple-element.135), channel_id=1, source_target_pairs={{0,3},{1,0},{2,1},{3,2},{4,7},{5,4},{6,5},{7,6},{8,11},{9,8},{10,9... | collective-permute-start | bytes 798728 | tf_op jit(solution)/shard_map/ppermute | solution.py:493
  20.2 2.4 %shard_map.91.refs_0_.refs_3_.refs_2_ = f32[1032,128]{1,0:T(8,128)S(1)} custom-call(s32[65]{0:T(128)S(1)} %get-tuple-element.119.refs_0_.refs_2_, s32[65]{0:T(128)S(1)} %get-tuple-element.120.refs_1_.refs_3_, s32[32]{0:T(128)S(1)} %get-tuple-element.121.refs_2_.refs_4_, f32[16,32]{1,0:T(8,128)S(1)} %get-tuple-element.122.refs_3_.refs_5_, ...), custom_call_target="tpu_custom_call" | custom-call | tf_op jit(solution)/shard_map/pallas_call | solution.py:476
  22.6 7.6 %collective-permute-done.17.refs_3_.refs_6_.refs_5_ = f32[264,128]{1,0:T(8,128)S(1)} collective-permute-done((f32[264,128]{1,0:T(8,128)S(1)}, f32[264,128]{1,0:T(8,128)S(1)}, u32[]{:S(2)}, u32[]{:S(2)}) %collective-permute-start.17) | collective-permute-done | bytes 135200 | tf_op jit(solution)/shard_map/ppermute | solution.py:493
  30.2 3.0 %shard_map.93 = (f32[904,128]{1,0:T(8,128)S(1)}, f32[904,128]{1,0:T(8,128)S(1)}, s32[235]{0:T(256)S(1)}, f32[8,128]{1,0:T(8,128)S(1)}) custom-call(f32[1032,128]{1,0:T(8,128)S(1)} %shard_map.91.refs_0_.refs_3_.refs_2_, f32[264,128]{1,0:T(8,128)S(1)} %collective-permute-done.15.refs_1_.refs_4_.refs_3_, ...), custom_call_target="tpu_custom_call" | custom-call | tf_op jit(solution)/shard_map/pallas_call | solution.py:525
  33.2 1.9 %collective-permute-start.27 = (f32[904,128]{1,0:T(8,128)S(1)}, f32[904,128]{1,0:T(8,128)S(1)}, u32[]{:S(2)}, u32[]{:S(2)}) collective-permute-start(f32[904,128]{1,0:T(8,128)S(1)} %get-tuple-element.141), channel_id=1, source_target_pairs={{4,0},{8,4},{12,8},{16,12},{20,16},{24,20},{28,24},{5,1},{9,5},{13... | collective-permute-start | bytes 1388552 | tf_op jit(solution)/shard_map/ppermute | solution.py:497
  35.1 0.6 collective-permute-start.18
  35.7 1.2 %collective-permute-done.18.refs_1_ = f32[8,128]{1,0:T(8,128)S(1)} collective-permute-done((f32[8,128]{1,0:T(8,128)S(1)}, f32[8,128]{1,0:T(8,128)S(1)}, u32[]{:S(2)}, u32[]{:S(2)}) %collective-permute-start.18) | collective-permute-done | bytes 4128 | tf_op jit(solution)/shard_map/ppermute | solution.py:502
  36.9 3.9 %shard_map.94 = (f32[264,128]{1,0:T(8,128)S(1)}, f32[264,128]{1,0:T(8,128)S(1)}, f32[264,128]{1,0:T(8,128)S(1)}, f32[8,128]{1,0:T(8,128)S(1)}) custom-call(f32[8,128]{1,0:T(8,128)S(1)} %get-tuple-element.131.refs_0_, f32[8,128]{1,0:T(8,128)S(1)} %collective-permute-done.18.refs_1_, s32[65]{0:T(128)S(1)} %get-tuple-element.119.refs_0_.refs_2_, ...), custom_call_target="tpu_custom_call" | custom-call | tf_op jit(solution)/shard_map/pallas_call | solution.py:476
  40.8 1.7 %collective-permute-start.19 = (f32[8,128]{1,0:T(8,128)S(1)}, f32[8,128]{1,0:T(8,128)S(1)}, u32[]{:S(2)}, u32[]{:S(2)}) collective-permute-start(f32[8,128]{1,0:T(8,128)S(1)} %get-tuple-element.132.refs_1_), channel_id=1, source_target_pairs={{0,8},{4,12},{8,0},{12,4},{16,24},{20,28},{24,16},{28,20},{1,9},{5... | collective-permute-start | bytes 12296 | tf_op jit(solution)/shard_map/ppermute | solution.py:502
  42.6 1.9 %collective-permute-done.19.refs_2_ = f32[8,128]{1,0:T(8,128)S(1)} collective-permute-done((f32[8,128]{1,0:T(8,128)S(1)}, f32[8,128]{1,0:T(8,128)S(1)}, u32[]{:S(2)}, u32[]{:S(2)}) %collective-permute-start.19) | collective-permute-done | bytes 4128 | tf_op jit(solution)/shard_map/ppermute | solution.py:502
  44.5 3.6 %collective-permute-start.24 = (f32[264,128]{1,0:T(8,128)S(1)}, f32[264,128]{1,0:T(8,128)S(1)}, u32[]{:S(2)}, u32[]{:S(2)}) collective-permute-start(f32[264,128]{1,0:T(8,128)S(1)} %get-tuple-element.137), channel_id=1, source_target_pairs={{0,1},{1,2},{2,3},{3,0},{4,5},{5,6},{6,7},{7,4},{8,9},{9,10},{10,1... | collective-permute-start | bytes 405512 | tf_op jit(solution)/shard_map/ppermute | solution.py:493
  48.1 3.6 %collective-permute-start.25 = (f32[264,128]{1,0:T(8,128)S(1)}, f32[264,128]{1,0:T(8,128)S(1)}, u32[]{:S(2)}, u32[]{:S(2)}) collective-permute-start(f32[264,128]{1,0:T(8,128)S(1)} %get-tuple-element.138), channel_id=1, source_target_pairs={{0,2},{1,3},{2,0},{3,1},{4,6},{5,7},{6,4},{7,5},{8,10},{9,11},{10,... | collective-permute-start | bytes 405512 | tf_op jit(solution)/shard_map/ppermute | solution.py:493
  51.7 0.7 shard_map.96
  52.4 0.6 collective-permute-start.23
  53.0 1.9 %collective-permute-start.28 = (f32[904,128]{1,0:T(8,128)S(1)}, f32[904,128]{1,0:T(8,128)S(1)}, u32[]{:S(2)}, u32[]{:S(2)}) collective-permute-start(f32[904,128]{1,0:T(8,128)S(1)} %get-tuple-element.142), channel_id=1, source_target_pairs={{0,4},{4,8},{8,12},{12,16},{16,20},{20,24},{24,28},{1,5},{5,9},{9,... | collective-permute-start | bytes 1388552 | tf_op jit(solution)/shard_map/ppermute | solution.py:497
  55.0 1.1 %collective-permute-done.23.refs_2_ = f32[8,128]{1,0:T(8,128)S(1)} collective-permute-done((f32[8,128]{1,0:T(8,128)S(1)}, f32[8,128]{1,0:T(8,128)S(1)}, u32[]{:S(2)}, u32[]{:S(2)}) %collective-permute-start.23) | collective-permute-done | bytes 4128 | tf_op jit(solution)/shard_map/ppermute | solution.py:502
  56.1 3.4 %collective-permute-start.29 = (f32[904,128]{1,0:T(8,128)S(1)}, f32[904,128]{1,0:T(8,128)S(1)}, u32[]{:S(2)}, u32[]{:S(2)}) collective-permute-start(f32[904,128]{1,0:T(8,128)S(1)} %get-tuple-element.145), channel_id=1, source_target_pairs={{4,0},{8,4},{12,8},{16,12},{20,16},{24,20},{28,24},{5,1},{9,5},{13... | collective-permute-start | bytes 1388552 | tf_op jit(solution)/shard_map/ppermute | solution.py:497
  59.5 1.9 %collective-permute-start.30 = (f32[904,128]{1,0:T(8,128)S(1)}, f32[904,128]{1,0:T(8,128)S(1)}, u32[]{:S(2)}, u32[]{:S(2)}) collective-permute-start(f32[904,128]{1,0:T(8,128)S(1)} %get-tuple-element.146), channel_id=1, source_target_pairs={{0,4},{4,8},{8,12},{12,16},{16,20},{20,24},{24,28},{1,5},{5,9},{9,... | collective-permute-start | bytes 1388552 | tf_op jit(solution)/shard_map/ppermute | solution.py:497
  61.5 6.2 %collective-permute-done.26.refs_12_.refs_11_ = f32[264,128]{1,0:T(8,128)S(1)} collective-permute-done((f32[264,128]{1,0:T(8,128)S(1)}, f32[264,128]{1,0:T(8,128)S(1)}, u32[]{:S(2)}, u32[]{:S(2)}) %collective-permute-start.26) | collective-permute-done | bytes 135200 | tf_op jit(solution)/shard_map/ppermute | solution.py:493
  67.8 0.8 shard_map.97
  68.5 2.8 %collective-permute-start.31 = (f32[392,128]{1,0:T(8,128)S(1)}, f32[392,128]{1,0:T(8,128)S(1)}, u32[]{:S(2)}, u32[]{:S(2)}) collective-permute-start(f32[392,128]{1,0:T(8,128)S(1)} %get-tuple-element.147), channel_id=1, source_target_pairs={{4,0},{8,4},{12,8},{16,12},{20,16},{24,20},{28,24},{5,1},{9,5},{13... | collective-permute-start | bytes 602120 | tf_op jit(solution)/shard_map/ppermute | solution.py:497
  71.3 1.9 %collective-permute-start.32 = (f32[392,128]{1,0:T(8,128)S(1)}, f32[392,128]{1,0:T(8,128)S(1)}, u32[]{:S(2)}, u32[]{:S(2)}) collective-permute-start(f32[392,128]{1,0:T(8,128)S(1)} %get-tuple-element.148), channel_id=1, source_target_pairs={{0,4},{4,8},{8,12},{12,16},{16,20},{20,24},{24,28},{1,5},{5,9},{9,... | collective-permute-start | bytes 602120 | tf_op jit(solution)/shard_map/ppermute | solution.py:497
  73.3 2.0 %settle.3 = (f32[48,64,128]{2,1,0:T(8,128)S(1)}, s32[1]{0:T(128)}) custom-call(s32[235]{0:T(256)S(1)} %get-tuple-element.130.refs_0_, f32[8,128]{1,0:T(8,128)S(1)} %get-tuple-element.140.refs_1_, f32[1032,128]{1,0:T(8,128)S(1)} %shard_map.91.refs_0_.refs_3_.refs_2_, f32[264,128]{1,0:T(8,128)S(1)} %collective-permute-done.15.refs_1_.refs_4_.refs_3_, ...), custom_call_target="tpu_custom_call" | custom-call | tf_op jit(solution)/shard_map/settle/pallas_call | solution.py:544
  75.9 3.3 %collective-permute-done.32.refs_4_ = f32[392,128]{1,0:T(8,128)S(1)} collective-permute-done((f32[392,128]{1,0:T(8,128)S(1)}, f32[392,128]{1,0:T(8,128)S(1)}, u32[]{:S(2)}, u32[]{:S(2)}) %collective-permute-start.32) | collective-permute-done | bytes 200736 | tf_op jit(solution)/shard_map/ppermute | solution.py:497
  79.3 1.8 %finish.3 = f32[48,64,128]{2,1,0:T(8,128)} custom-call(f32[48,64,128]{2,1,0:T(8,128)S(1)} %get-tuple-element.144.refs_0_, f32[904,128]{1,0:T(8,128)S(1)} %collective-permute-done.29.refs_1_, f32[904,128]{1,0:T(8,128)S(1)} %collective-permute-done.30.refs_2_, f32[392,128]{1,0:T(8,128)S(1)} %collective-permute-done.31.refs_3_, ...), custom_call_target="tpu_custom_call" | custom-call | tf_op jit(solution)/shard_map/finish/pallas_call | solution.py:554
  (15 shorter events, 0.3 us)
Async XLA Ops:
  7.8 10.8 %collective-permute-start.15 = (f32[264,128]{1,0:T(8,128)S(1)}, f32[264,128]{1,0:T(8,128)S(1)}, u32[]{:S(2)}, u32[]{:S(2)}) collective-permute-start(f32[264,128]{1,0:T(8,128)S(1)} %get-tuple-element.127), channel_id=1, source_target_pairs={{0,1},{1,2},{2,3},{3,0},{4,5},{5,6},{6,7},{7,4},{8,9},{9,10},{10,1... | collective-permute-start | bytes 405512 | tf_op jit(solution)/shard_map/ppermute | solution.py:493
  9.4 20.8 %collective-permute-start.17 = (f32[264,128]{1,0:T(8,128)S(1)}, f32[264,128]{1,0:T(8,128)S(1)}, u32[]{:S(2)}, u32[]{:S(2)}) collective-permute-start(f32[264,128]{1,0:T(8,128)S(1)} %get-tuple-element.129), channel_id=1, source_target_pairs={{0,3},{1,0},{2,1},{3,2},{4,7},{5,4},{6,5},{7,6},{8,11},{9,8},{10,9... | collective-permute-start | bytes 405512 | tf_op jit(solution)/shard_map/ppermute | solution.py:493
  9.9 20.3 %collective-permute-start.16 = (f32[264,128]{1,0:T(8,128)S(1)}, f32[264,128]{1,0:T(8,128)S(1)}, u32[]{:S(2)}, u32[]{:S(2)}) collective-permute-start(f32[264,128]{1,0:T(8,128)S(1)} %get-tuple-element.128), channel_id=1, source_target_pairs={{0,2},{1,3},{2,0},{3,1},{4,6},{5,7},{6,4},{7,5},{8,10},{9,11},{10,... | collective-permute-start | bytes 405512 | tf_op jit(solution)/shard_map/ppermute | solution.py:493
  16.8 31.3 %collective-permute-start.20 = (f32[520,128]{1,0:T(8,128)S(1)}, f32[520,128]{1,0:T(8,128)S(1)}, u32[]{:S(2)}, u32[]{:S(2)}) collective-permute-start(f32[520,128]{1,0:T(8,128)S(1)} %get-tuple-element.133), channel_id=1, source_target_pairs={{0,1},{1,2},{2,3},{3,0},{4,5},{5,6},{6,7},{7,4},{8,9},{9,10},{10,1... | collective-permute-start | bytes 798728 | tf_op jit(solution)/shard_map/ppermute | solution.py:493
  18.6 33.1 %collective-permute-start.21 = (f32[520,128]{1,0:T(8,128)S(1)}, f32[520,128]{1,0:T(8,128)S(1)}, u32[]{:S(2)}, u32[]{:S(2)}) collective-permute-start(f32[520,128]{1,0:T(8,128)S(1)} %get-tuple-element.134), channel_id=1, source_target_pairs={{0,2},{1,3},{2,0},{3,1},{4,6},{5,7},{6,4},{7,5},{8,10},{9,11},{10,... | collective-permute-start | bytes 798728 | tf_op jit(solution)/shard_map/ppermute | solution.py:493
  18.6 33.1 %collective-permute-start.22 = (f32[520,128]{1,0:T(8,128)S(1)}, f32[520,128]{1,0:T(8,128)S(1)}, u32[]{:S(2)}, u32[]{:S(2)}) collective-permute-start(f32[520,128]{1,0:T(8,128)S(1)} %get-tuple-element.135), channel_id=1, source_target_pairs={{0,3},{1,0},{2,1},{3,2},{4,7},{5,4},{6,5},{7,6},{8,11},{9,8},{10,9... | collective-permute-start | bytes 798728 | tf_op jit(solution)/shard_map/ppermute | solution.py:493
  33.2 38.2 %collective-permute-start.27 = (f32[904,128]{1,0:T(8,128)S(1)}, f32[904,128]{1,0:T(8,128)S(1)}, u32[]{:S(2)}, u32[]{:S(2)}) collective-permute-start(f32[904,128]{1,0:T(8,128)S(1)} %get-tuple-element.141), channel_id=1, source_target_pairs={{4,0},{8,4},{12,8},{16,12},{20,16},{24,20},{28,24},{5,1},{9,5},{13... | collective-permute-start | bytes 1388552 | tf_op jit(solution)/shard_map/ppermute | solution.py:497
  35.1 1.8 %collective-permute-start.18 = (f32[8,128]{1,0:T(8,128)S(1)}, f32[8,128]{1,0:T(8,128)S(1)}, u32[]{:S(2)}, u32[]{:S(2)}) collective-permute-start(f32[8,128]{1,0:T(8,128)S(1)} %get-tuple-element.131.refs_0_), channel_id=1, source_target_pairs={{0,4},{4,0},{8,12},{12,8},{16,20},{20,16},{24,28},{28,24},{1,5},{5... | collective-permute-start | bytes 12296 | tf_op jit(solution)/shard_map/ppermute | solution.py:502
  40.8 3.7 %collective-permute-start.19 = (f32[8,128]{1,0:T(8,128)S(1)}, f32[8,128]{1,0:T(8,128)S(1)}, u32[]{:S(2)}, u32[]{:S(2)}) collective-permute-start(f32[8,128]{1,0:T(8,128)S(1)} %get-tuple-element.132.refs_1_), channel_id=1, source_target_pairs={{0,8},{4,12},{8,0},{12,4},{16,24},{20,28},{24,16},{28,20},{1,9},{5... | collective-permute-start | bytes 12296 | tf_op jit(solution)/shard_map/ppermute | solution.py:502
  44.5 15.0 %collective-permute-start.24 = (f32[264,128]{1,0:T(8,128)S(1)}, f32[264,128]{1,0:T(8,128)S(1)}, u32[]{:S(2)}, u32[]{:S(2)}) collective-permute-start(f32[264,128]{1,0:T(8,128)S(1)} %get-tuple-element.137), channel_id=1, source_target_pairs={{0,1},{1,2},{2,3},{3,0},{4,5},{5,6},{6,7},{7,4},{8,9},{9,10},{10,1... | collective-permute-start | bytes 405512 | tf_op jit(solution)/shard_map/ppermute | solution.py:493
  48.1 13.3 %collective-permute-start.25 = (f32[264,128]{1,0:T(8,128)S(1)}, f32[264,128]{1,0:T(8,128)S(1)}, u32[]{:S(2)}, u32[]{:S(2)}) collective-permute-start(f32[264,128]{1,0:T(8,128)S(1)} %get-tuple-element.138), channel_id=1, source_target_pairs={{0,2},{1,3},{2,0},{3,1},{4,6},{5,7},{6,4},{7,5},{8,10},{9,11},{10,... | collective-permute-start | bytes 405512 | tf_op jit(solution)/shard_map/ppermute | solution.py:493
  52.4 3.7 %collective-permute-start.23 = (f32[8,128]{1,0:T(8,128)S(1)}, f32[8,128]{1,0:T(8,128)S(1)}, u32[]{:S(2)}, u32[]{:S(2)}) collective-permute-start(f32[8,128]{1,0:T(8,128)S(1)} %get-tuple-element.136.refs_1_), channel_id=1, source_target_pairs={{0,16},{4,20},{8,24},{12,28},{16,0},{20,4},{24,8},{28,12},{1,17},{... | collective-permute-start | bytes 12296 | tf_op jit(solution)/shard_map/ppermute | solution.py:502
  53.0 20.2 %collective-permute-start.28 = (f32[904,128]{1,0:T(8,128)S(1)}, f32[904,128]{1,0:T(8,128)S(1)}, u32[]{:S(2)}, u32[]{:S(2)}) collective-permute-start(f32[904,128]{1,0:T(8,128)S(1)} %get-tuple-element.142), channel_id=1, source_target_pairs={{0,4},{4,8},{8,12},{12,16},{16,20},{20,24},{24,28},{1,5},{5,9},{9,... | collective-permute-start | bytes 1388552 | tf_op jit(solution)/shard_map/ppermute | solution.py:497
  56.1 23.2 %collective-permute-start.29 = (f32[904,128]{1,0:T(8,128)S(1)}, f32[904,128]{1,0:T(8,128)S(1)}, u32[]{:S(2)}, u32[]{:S(2)}) collective-permute-start(f32[904,128]{1,0:T(8,128)S(1)} %get-tuple-element.145), channel_id=1, source_target_pairs={{4,0},{8,4},{12,8},{16,12},{20,16},{24,20},{28,24},{5,1},{9,5},{13... | collective-permute-start | bytes 1388552 | tf_op jit(solution)/shard_map/ppermute | solution.py:497
  59.5 19.8 %collective-permute-start.30 = (f32[904,128]{1,0:T(8,128)S(1)}, f32[904,128]{1,0:T(8,128)S(1)}, u32[]{:S(2)}, u32[]{:S(2)}) collective-permute-start(f32[904,128]{1,0:T(8,128)S(1)} %get-tuple-element.146), channel_id=1, source_target_pairs={{0,4},{4,8},{8,12},{12,16},{16,20},{20,24},{24,28},{1,5},{5,9},{9,... | collective-permute-start | bytes 1388552 | tf_op jit(solution)/shard_map/ppermute | solution.py:497
  61.5 6.3 %collective-permute-start.26 = (f32[264,128]{1,0:T(8,128)S(1)}, f32[264,128]{1,0:T(8,128)S(1)}, u32[]{:S(2)}, u32[]{:S(2)}) collective-permute-start(f32[264,128]{1,0:T(8,128)S(1)} %get-tuple-element.139), channel_id=1, source_target_pairs={{0,3},{1,0},{2,1},{3,2},{4,7},{5,4},{6,5},{7,6},{8,11},{9,8},{10,9... | collective-permute-start | bytes 405512 | tf_op jit(solution)/shard_map/ppermute | solution.py:493
  68.5 7.4 %collective-permute-start.31 = (f32[392,128]{1,0:T(8,128)S(1)}, f32[392,128]{1,0:T(8,128)S(1)}, u32[]{:S(2)}, u32[]{:S(2)}) collective-permute-start(f32[392,128]{1,0:T(8,128)S(1)} %get-tuple-element.147), channel_id=1, source_target_pairs={{4,0},{8,4},{12,8},{16,12},{20,16},{24,20},{28,24},{5,1},{9,5},{13... | collective-permute-start | bytes 602120 | tf_op jit(solution)/shard_map/ppermute | solution.py:497
  71.3 7.9 %collective-permute-start.32 = (f32[392,128]{1,0:T(8,128)S(1)}, f32[392,128]{1,0:T(8,128)S(1)}, u32[]{:S(2)}, u32[]{:S(2)}) collective-permute-start(f32[392,128]{1,0:T(8,128)S(1)} %get-tuple-element.148), channel_id=1, source_target_pairs={{0,4},{4,8},{8,12},{12,16},{16,20},{20,24},{24,28},{1,5},{5,9},{9,... | collective-permute-start | bytes 602120 | tf_op jit(solution)/shard_map/ppermute | solution.py:497
where the time goes:
time: 81.8 us; the launch traced here: 81.5 us
  starting transfers between devices  31.5 us (39%)
  Pallas kernels  27.2 us (33%)
  waiting for transfers between devices  21.5 us (26%)
  between operations  1.02 us (1%)
    pallas_call x4, Pallas kernels, more(): pl.pallas_call(functools.partial(resample_kernel, cfg, False, parts, bool...  15.1 us
    ppermute x9, starting transfers between devices, turn(): lax.ppermute(x, 'epoch', [(i, (i + d) % epochs) for i in range(epochs)])  14.7 us
    ppermute x6, starting transfers between devices, beside(): return lax.ppermute(x, 'tile', route)  13.9 us
    ppermute x9, waiting for transfers between devices, turn(): lax.ppermute(x, 'epoch', [(i, (i + d) % epochs) for i in range(epochs)])  13.9 us
    pallas_call x3, Pallas kernels, run(): pl.pallas_call(functools.partial(collect_kernel, cfg, queues, k, ends), o...  4.4 us
    ppermute x3, waiting for transfers between devices, swap(): return lax.ppermute(x, 'tile', [(i, i ^ 1 << k) for i in range(tiles)])  4.29 us
    pallas_call x1, Pallas kernels, run(): pl.pallas_call(functools.partial(resample_kernel, cfg, True, [(middle, st...  3.92 us
    ppermute x6, waiting for transfers between devices, beside(): return lax.ppermute(x, 'tile', route)  3.35 us
  transfers between devices with their start and end apart: 18, of which 6 were waited for; matrix products, arithmetic and copies ran while one was open for 0% of the time, Pallas kernels for 22%

commit v1 on v0

--- a/solution.py
+++ b/solution.py
@@ -222,15 +222,13 @@
         work(4 * quads, 1)
 
 
-def read_heads(sources, head_refs, sems, meanwhile=None):
+def read_heads(sources, head_refs, sems):
     copies = [
         pltpu.make_async_copy(src.at[pl.ds(src.shape[0] - HEAD, 1)], dst, sems.at[i])
         for i, (src, dst) in enumerate(zip(sources, head_refs))
     ]
     for copy in copies:
         copy.start()
-    if meanwhile is not None:
-        meanwhile()
     for copy in copies:
         copy.wait()
 
@@ -398,11 +396,8 @@
     waves = (len(refs) - 3) // 2
     total_ref, sources, out_ref = refs[0], refs[1 : 1 + waves], refs[1 + waves]
     head_refs, sems = refs[2 + waves : -1], refs[-1]
-
-    def take_over():
-        out_ref[...] = total_ref[...]
-
-    read_heads(sources, head_refs, sems, take_over)
+    out_ref[...] = total_ref[...]
+    read_heads(sources, head_refs, sems)
     add_waves(out_ref, sources, head_refs, rows)
 
 
@@ -574,7 +569,7 @@
     ]
     sends = full
     if capacity >= 16 and tiles == 1 << len(full):
-        sends = [7 * capacity // 8, 7 * capacity // 8, 3 * capacity // 8]
+        sends = [13 * capacity // 16, 7 * capacity // 8, 3 * capacity // 8]
         sends = [min(a, b) for a, b in zip(sends, full)]
     out, failed = run(cfg, sends, args)
     if failed is not None:

time: 81.8 us -> 80.6 us (0.985)
  the two profiles are of different devices: /device:TPU:12 before, /device:TPU:1 now
where the time goes in v1:
time: 80.6 us; the launch traced here: 79.7 us
  starting transfers between devices  35.1 us (44%)
  Pallas kernels  28.6 us (35%)
  waiting for transfers between devices  14.8 us (18%)
  between operations  1.07 us (1%)
    ppermute x6, starting transfers between devices, beside(): return lax.ppermute(x, 'tile', route)  18 us
    pallas_call x4, Pallas kernels, more(): pl.pallas_call(functools.partial(resample_kernel, cfg, False, parts, bool...  15.2 us
    ppermute x9, starting transfers between devices, turn(): lax.ppermute(x, 'epoch', [(i, (i + d) % epochs) for i in range(epochs)])  13.5 us
    ppermute x9, waiting for transfers between devices, turn(): lax.ppermute(x, 'epoch', [(i, (i + d) % epochs) for i in range(epochs)])  12.4 us
    pallas_call x3, Pallas kernels, run(): pl.pallas_call(functools.partial(collect_kernel, cfg, queues, k, ends), o...  5.03 us
    pallas_call x1, Pallas kernels, run(): pl.pallas_call(functools.partial(resample_kernel, cfg, True, [(middle, st...  3.92 us
    ppermute x3, starting transfers between devices, swap(): return lax.ppermute(x, 'tile', [(i, i ^ 1 << k) for i in range(tiles)])  3.56 us
    pallas_call x1, Pallas kernels, run(): pl.pallas_call(functools.partial(settle_kernel, cfg, queues), out_shape=[...  2.43 us
  transfers between devices with their start and end apart: 18, of which 4 were waited for; matrix products, arithmetic and copies ran while one was open for 0% of the time, Pallas kernels for 24%

profile of v1, /device:TPU:1, one launch (start us, length us, event | category | flops | bytes accessed | tf_op | source)
XLA Modules:
  0.0 79.7 jit_solution(13027543327622820079)
XLA Ops:
  0.0 3.9 %resample_first.3 = (f32[264,128]{1,0:T(8,128)S(1)}, bf16[2048,256]{1,0:T(8,128)(2,1)S(1)}, bf16[1024,256]{1,0:T(8,128)(2,1)S(1)}, bf16[32,64,128]{2,1,0:T(8,128...) custom-call(s32[32]{0:T(128)} %bitcast.26, ...), custom_call_target="tpu_custom_call" | custom-call | tf_op jit(solution)/shard_map/resample_first/pallas_call | solution.py:455
  3.9 3.3 %shard_map.92 = (f32[264,128]{1,0:T(8,128)S(1)}, f32[264,128]{1,0:T(8,128)S(1)}) custom-call(s32[65]{0:T(128)S(1)} %get-tuple-element.119.refs_0_.refs_2_, s32[65]{0:T(128)S(1)} %get-tuple-element.120.refs_1_.refs_3_, s32[32]{0:T(128)S(1)} %get-tuple-element.121.refs_2_.refs_4_, f32[16,32]{1,0:T(8,128)S(1)} %get-tuple-element.122.refs_3_.refs_5_, ...), custom_call_target="tpu_custom_call" | custom-call | tf_op jit(solution)/shard_map/pallas_call | solution.py:471
  7.2 2.2 %collective-permute-start.15 = (f32[264,128]{1,0:T(8,128)S(1)}, f32[264,128]{1,0:T(8,128)S(1)}, u32[]{:S(2)}, u32[]{:S(2)}) collective-permute-start(f32[264,128]{1,0:T(8,128)S(1)} %get-tuple-element.127), channel_id=1, source_target_pairs={{0,1},{1,2},{2,3},{3,0},{4,5},{5,6},{6,7},{7,4},{8,9},{9,10},{10,1... | collective-permute-start | bytes 405512 | tf_op jit(solution)/shard_map/ppermute | solution.py:488
  9.4 2.1 %collective-permute-start.17 = (f32[264,128]{1,0:T(8,128)S(1)}, f32[264,128]{1,0:T(8,128)S(1)}, u32[]{:S(2)}, u32[]{:S(2)}) collective-permute-start(f32[264,128]{1,0:T(8,128)S(1)} %get-tuple-element.129), channel_id=1, source_target_pairs={{0,3},{1,0},{2,1},{3,2},{4,7},{5,4},{6,5},{7,6},{8,11},{9,8},{10,9... | collective-permute-start | bytes 405512 | tf_op jit(solution)/shard_map/ppermute | solution.py:488
  11.5 0.4 collective-permute-start.16
  11.9 1.8 %shard_map.95 = (f32[520,128]{1,0:T(8,128)S(1)}, f32[520,128]{1,0:T(8,128)S(1)}, f32[520,128]{1,0:T(8,128)S(1)}) custom-call(s32[65]{0:T(128)S(1)} %get-tuple-element.119.refs_0_.refs_2_, s32[65]{0:T(128)S(1)} %get-tuple-element.120.refs_1_.refs_3_, s32[32]{0:T(128)S(1)} %get-tuple-element.121.refs_2_.refs_4_, ...), custom_call_target="tpu_custom_call" | custom-call | tf_op jit(solution)/shard_map/pallas_call | solution.py:471
  13.7 3.5 %collective-permute-start.20 = (f32[520,128]{1,0:T(8,128)S(1)}, f32[520,128]{1,0:T(8,128)S(1)}, u32[]{:S(2)}, u32[]{:S(2)}) collective-permute-start(f32[520,128]{1,0:T(8,128)S(1)} %get-tuple-element.133), channel_id=1, source_target_pairs={{0,1},{1,2},{2,3},{3,0},{4,5},{5,6},{6,7},{7,4},{8,9},{9,10},{10,1... | collective-permute-start | bytes 798728 | tf_op jit(solution)/shard_map/ppermute | solution.py:488
  17.3 0.8 collective-permute-start.21
  18.0 0.0 collective-permute-done.15.refs_1_.refs_4_.refs_3_
  18.0 2.3 %collective-permute-start.22 = (f32[520,128]{1,0:T(8,128)S(1)}, f32[520,128]{1,0:T(8,128)S(1)}, u32[]{:S(2)}, u32[]{:S(2)}) collective-permute-start(f32[520,128]{1,0:T(8,128)S(1)} %get-tuple-element.135), channel_id=1, source_target_pairs={{0,3},{1,0},{2,1},{3,2},{4,7},{5,4},{6,5},{7,6},{8,11},{9,8},{10,9... | collective-permute-start | bytes 798728 | tf_op jit(solution)/shard_map/ppermute | solution.py:488
  20.3 6.8 %shard_map.91.refs_0_.refs_3_.refs_2_ = f32[1032,128]{1,0:T(8,128)S(1)} custom-call(s32[65]{0:T(128)S(1)} %get-tuple-element.119.refs_0_.refs_2_, s32[65]{0:T(128)S(1)} %get-tuple-element.120.refs_1_.refs_3_, s32[32]{0:T(128)S(1)} %get-tuple-element.121.refs_2_.refs_4_, f32[16,32]{1,0:T(8,128)S(1)} %get-tuple-element.122.refs_3_.refs_5_, ...), custom_call_target="tpu_custom_call" | custom-call | tf_op jit(solution)/shard_map/pallas_call | solution.py:471
  27.1 8.5 %collective-permute-done.16.refs_2_.refs_5_.refs_4_ = f32[264,128]{1,0:T(8,128)S(1)} collective-permute-done((f32[264,128]{1,0:T(8,128)S(1)}, f32[264,128]{1,0:T(8,128)S(1)}, u32[]{:S(2)}, u32[]{:S(2)}) %collective-permute-start.16) | collective-permute-done | bytes 135200 | tf_op jit(solution)/shard_map/ppermute | solution.py:488
  35.6 3.1 %shard_map.93 = (f32[840,128]{1,0:T(8,128)S(1)}, f32[840,128]{1,0:T(8,128)S(1)}, s32[235]{0:T(256)S(1)}, f32[8,128]{1,0:T(8,128)S(1)}) custom-call(f32[1032,128]{1,0:T(8,128)S(1)} %shard_map.91.refs_0_.refs_3_.refs_2_, f32[264,128]{1,0:T(8,128)S(1)} %collective-permute-done.15.refs_1_.refs_4_.refs_3_, ...), custom_call_target="tpu_custom_call" | custom-call | tf_op jit(solution)/shard_map/pallas_call | solution.py:520
  38.7 2.2 %collective-permute-start.27 = (f32[840,128]{1,0:T(8,128)S(1)}, f32[840,128]{1,0:T(8,128)S(1)}, u32[]{:S(2)}, u32[]{:S(2)}) collective-permute-start(f32[840,128]{1,0:T(8,128)S(1)} %get-tuple-element.141), channel_id=1, source_target_pairs={{4,0},{8,4},{12,8},{16,12},{20,16},{24,20},{28,24},{5,1},{9,5},{13... | collective-permute-start | bytes 1290248 | tf_op jit(solution)/shard_map/ppermute | solution.py:492
  41.0 0.1 collective-permute-start.18
  41.1 1.3 %collective-permute-done.18.refs_1_ = f32[8,128]{1,0:T(8,128)S(1)} collective-permute-done((f32[8,128]{1,0:T(8,128)S(1)}, f32[8,128]{1,0:T(8,128)S(1)}, u32[]{:S(2)}, u32[]{:S(2)}) %collective-permute-start.18) | collective-permute-done | bytes 4128 | tf_op jit(solution)/shard_map/ppermute | solution.py:497
  42.4 3.3 %shard_map.94 = (f32[264,128]{1,0:T(8,128)S(1)}, f32[264,128]{1,0:T(8,128)S(1)}, f32[264,128]{1,0:T(8,128)S(1)}, f32[8,128]{1,0:T(8,128)S(1)}) custom-call(f32[8,128]{1,0:T(8,128)S(1)} %get-tuple-element.131.refs_0_, f32[8,128]{1,0:T(8,128)S(1)} %collective-permute-done.18.refs_1_, s32[65]{0:T(128)S(1)} %get-tuple-element.119.refs_0_.refs_2_, ...), custom_call_target="tpu_custom_call" | custom-call | tf_op jit(solution)/shard_map/pallas_call | solution.py:471
  45.7 2.4 %collective-permute-start.19 = (f32[8,128]{1,0:T(8,128)S(1)}, f32[8,128]{1,0:T(8,128)S(1)}, u32[]{:S(2)}, u32[]{:S(2)}) collective-permute-start(f32[8,128]{1,0:T(8,128)S(1)} %get-tuple-element.132.refs_1_), channel_id=1, source_target_pairs={{0,8},{4,12},{8,0},{12,4},{16,24},{20,28},{24,16},{28,20},{1,9},{5... | collective-permute-start | bytes 12296 | tf_op jit(solution)/shard_map/ppermute | solution.py:497
  48.1 1.0 %collective-permute-done.19.refs_2_ = f32[8,128]{1,0:T(8,128)S(1)} collective-permute-done((f32[8,128]{1,0:T(8,128)S(1)}, f32[8,128]{1,0:T(8,128)S(1)}, u32[]{:S(2)}, u32[]{:S(2)}) %collective-permute-start.19) | collective-permute-done | bytes 4128 | tf_op jit(solution)/shard_map/ppermute | solution.py:497
  49.1 1.2 %shard_map.96 = (f32[904,128]{1,0:T(8,128)S(1)}, f32[904,128]{1,0:T(8,128)S(1)}, f32[8,128]{1,0:T(8,128)S(1)}) custom-call(s32[235]{0:T(256)S(1)} %get-tuple-element.130.refs_0_, f32[8,128]{1,0:T(8,128)S(1)} %get-tuple-element.132.refs_1_, f32[8,128]{1,0:T(8,128)S(1)} %collective-permute-done.19.refs_2_, f32[1032,128]{1,0:T(8,128)S(1)} %shard_map.91.refs_0_.refs_3_.refs_2_, ...), custom_call_target="tpu_custom_call" | custom-call | tf_op jit(solution)/shard_map/pallas_call | solution.py:520
  50.3 1.1 %collective-permute-start.23 = (f32[8,128]{1,0:T(8,128)S(1)}, f32[8,128]{1,0:T(8,128)S(1)}, u32[]{:S(2)}, u32[]{:S(2)}) collective-permute-start(f32[8,128]{1,0:T(8,128)S(1)} %get-tuple-element.136.refs_1_), channel_id=1, source_target_pairs={{0,16},{4,20},{8,24},{12,28},{16,0},{20,4},{24,8},{28,12},{1,17},{... | collective-permute-start | bytes 12296 | tf_op jit(solution)/shard_map/ppermute | solution.py:497
  51.4 3.8 %collective-permute-start.29 = (f32[904,128]{1,0:T(8,128)S(1)}, f32[904,128]{1,0:T(8,128)S(1)}, u32[]{:S(2)}, u32[]{:S(2)}) collective-permute-start(f32[904,128]{1,0:T(8,128)S(1)} %get-tuple-element.145), channel_id=1, source_target_pairs={{4,0},{8,4},{12,8},{16,12},{20,16},{24,20},{28,24},{5,1},{9,5},{13... | collective-permute-start | bytes 1388552 | tf_op jit(solution)/shard_map/ppermute | solution.py:492
  55.3 3.5 %collective-permute-start.30 = (f32[904,128]{1,0:T(8,128)S(1)}, f32[904,128]{1,0:T(8,128)S(1)}, u32[]{:S(2)}, u32[]{:S(2)}) collective-permute-start(f32[904,128]{1,0:T(8,128)S(1)} %get-tuple-element.146), channel_id=1, source_target_pairs={{0,4},{4,8},{8,12},{12,16},{16,20},{20,24},{24,28},{1,5},{5,9},{9,... | collective-permute-start | bytes 1388552 | tf_op jit(solution)/shard_map/ppermute | solution.py:492
  58.8 2.9 %collective-permute-start.28 = (f32[840,128]{1,0:T(8,128)S(1)}, f32[840,128]{1,0:T(8,128)S(1)}, u32[]{:S(2)}, u32[]{:S(2)}) collective-permute-start(f32[840,128]{1,0:T(8,128)S(1)} %get-tuple-element.142), channel_id=1, source_target_pairs={{0,4},{4,8},{8,12},{12,16},{16,20},{20,24},{24,28},{1,5},{5,9},{9,... | collective-permute-start | bytes 1290248 | tf_op jit(solution)/shard_map/ppermute | solution.py:492
  61.7 2.2 %collective-permute-start.26 = (f32[264,128]{1,0:T(8,128)S(1)}, f32[264,128]{1,0:T(8,128)S(1)}, u32[]{:S(2)}, u32[]{:S(2)}) collective-permute-start(f32[264,128]{1,0:T(8,128)S(1)} %get-tuple-element.139), channel_id=1, source_target_pairs={{0,3},{1,0},{2,1},{3,2},{4,7},{5,4},{6,5},{7,6},{8,11},{9,8},{10,9... | collective-permute-start | bytes 405512 | tf_op jit(solution)/shard_map/ppermute | solution.py:488
  63.9 3.9 %collective-permute-done.26.refs_12_.refs_11_ = f32[264,128]{1,0:T(8,128)S(1)} collective-permute-done((f32[264,128]{1,0:T(8,128)S(1)}, f32[264,128]{1,0:T(8,128)S(1)}, u32[]{:S(2)}, u32[]{:S(2)}) %collective-permute-start.26) | collective-permute-done | bytes 135200 | tf_op jit(solution)/shard_map/ppermute | solution.py:488
  67.8 0.8 shard_map.97
  68.6 3.0 %collective-permute-start.31 = (f32[392,128]{1,0:T(8,128)S(1)}, f32[392,128]{1,0:T(8,128)S(1)}, u32[]{:S(2)}, u32[]{:S(2)}) collective-permute-start(f32[392,128]{1,0:T(8,128)S(1)} %get-tuple-element.147), channel_id=1, source_target_pairs={{4,0},{8,4},{12,8},{16,12},{20,16},{24,20},{28,24},{5,1},{9,5},{13... | collective-permute-start | bytes 602120 | tf_op jit(solution)/shard_map/ppermute | solution.py:492
  71.6 2.6 %collective-permute-start.32 = (f32[392,128]{1,0:T(8,128)S(1)}, f32[392,128]{1,0:T(8,128)S(1)}, u32[]{:S(2)}, u32[]{:S(2)}) collective-permute-start(f32[392,128]{1,0:T(8,128)S(1)} %get-tuple-element.148), channel_id=1, source_target_pairs={{0,4},{4,8},{8,12},{12,16},{16,20},{20,24},{24,28},{1,5},{5,9},{9,... | collective-permute-start | bytes 602120 | tf_op jit(solution)/shard_map/ppermute | solution.py:492
  74.2 2.4 %settle.3 = (f32[48,64,128]{2,1,0:T(8,128)S(1)}, s32[1]{0:T(128)}) custom-call(s32[235]{0:T(256)S(1)} %get-tuple-element.130.refs_0_, f32[8,128]{1,0:T(8,128)S(1)} %get-tuple-element.140.refs_1_, f32[1032,128]{1,0:T(8,128)S(1)} %shard_map.91.refs_0_.refs_3_.refs_2_, f32[264,128]{1,0:T(8,128)S(1)} %collective-permute-done.15.refs_1_.refs_4_.refs_3_, ...), custom_call_target="tpu_custom_call" | custom-call | tf_op jit(solution)/shard_map/settle/pallas_call | solution.py:539
  77.3 2.0 %finish.3 = f32[48,64,128]{2,1,0:T(8,128)} custom-call(f32[48,64,128]{2,1,0:T(8,128)S(1)} %get-tuple-element.144.refs_0_, f32[904,128]{1,0:T(8,128)S(1)} %collective-permute-done.29.refs_1_, f32[904,128]{1,0:T(8,128)S(1)} %collective-permute-done.30.refs_2_, f32[392,128]{1,0:T(8,128)S(1)} %collective-permute-done.31.refs_3_, ...), custom_call_target="tpu_custom_call" | custom-call | tf_op jit(solution)/shard_map/finish/pallas_call | solution.py:549
  79.3 0.2 while.9
  (15 shorter events, 0.0 us)
Async XLA Ops:
  7.2 10.8 %collective-permute-start.15 = (f32[264,128]{1,0:T(8,128)S(1)}, f32[264,128]{1,0:T(8,128)S(1)}, u32[]{:S(2)}, u32[]{:S(2)}) collective-permute-start(f32[264,128]{1,0:T(8,128)S(1)} %get-tuple-element.127), channel_id=1, source_target_pairs={{0,1},{1,2},{2,3},{3,0},{4,5},{5,6},{6,7},{7,4},{8,9},{9,10},{10,1... | collective-permute-start | bytes 405512 | tf_op jit(solution)/shard_map/ppermute | solution.py:488
  9.4 17.7 %collective-permute-start.17 = (f32[264,128]{1,0:T(8,128)S(1)}, f32[264,128]{1,0:T(8,128)S(1)}, u32[]{:S(2)}, u32[]{:S(2)}) collective-permute-start(f32[264,128]{1,0:T(8,128)S(1)} %get-tuple-element.129), channel_id=1, source_target_pairs={{0,3},{1,0},{2,1},{3,2},{4,7},{5,4},{6,5},{7,6},{8,11},{9,8},{10,9... | collective-permute-start | bytes 405512 | tf_op jit(solution)/shard_map/ppermute | solution.py:488
  11.5 24.1 %collective-permute-start.16 = (f32[264,128]{1,0:T(8,128)S(1)}, f32[264,128]{1,0:T(8,128)S(1)}, u32[]{:S(2)}, u32[]{:S(2)}) collective-permute-start(f32[264,128]{1,0:T(8,128)S(1)} %get-tuple-element.128), channel_id=1, source_target_pairs={{0,2},{1,3},{2,0},{3,1},{4,6},{5,7},{6,4},{7,5},{8,10},{9,11},{10,... | collective-permute-start | bytes 405512 | tf_op jit(solution)/shard_map/ppermute | solution.py:488
  13.7 35.4 %collective-permute-start.20 = (f32[520,128]{1,0:T(8,128)S(1)}, f32[520,128]{1,0:T(8,128)S(1)}, u32[]{:S(2)}, u32[]{:S(2)}) collective-permute-start(f32[520,128]{1,0:T(8,128)S(1)} %get-tuple-element.133), channel_id=1, source_target_pairs={{0,1},{1,2},{2,3},{3,0},{4,5},{5,6},{6,7},{7,4},{8,9},{9,10},{10,1... | collective-permute-start | bytes 798728 | tf_op jit(solution)/shard_map/ppermute | solution.py:488
  17.3 31.9 %collective-permute-start.21 = (f32[520,128]{1,0:T(8,128)S(1)}, f32[520,128]{1,0:T(8,128)S(1)}, u32[]{:S(2)}, u32[]{:S(2)}) collective-permute-start(f32[520,128]{1,0:T(8,128)S(1)} %get-tuple-element.134), channel_id=1, source_target_pairs={{0,2},{1,3},{2,0},{3,1},{4,6},{5,7},{6,4},{7,5},{8,10},{9,11},{10,... | collective-permute-start | bytes 798728 | tf_op jit(solution)/shard_map/ppermute | solution.py:488
  18.0 31.1 %collective-permute-start.22 = (f32[520,128]{1,0:T(8,128)S(1)}, f32[520,128]{1,0:T(8,128)S(1)}, u32[]{:S(2)}, u32[]{:S(2)}) collective-permute-start(f32[520,128]{1,0:T(8,128)S(1)} %get-tuple-element.135), channel_id=1, source_target_pairs={{0,3},{1,0},{2,1},{3,2},{4,7},{5,4},{6,5},{7,6},{8,11},{9,8},{10,9... | collective-permute-start | bytes 798728 | tf_op jit(solution)/shard_map/ppermute | solution.py:488
  38.7 32.8 %collective-permute-start.27 = (f32[840,128]{1,0:T(8,128)S(1)}, f32[840,128]{1,0:T(8,128)S(1)}, u32[]{:S(2)}, u32[]{:S(2)}) collective-permute-start(f32[840,128]{1,0:T(8,128)S(1)} %get-tuple-element.141), channel_id=1, source_target_pairs={{4,0},{8,4},{12,8},{16,12},{20,16},{24,20},{28,24},{5,1},{9,5},{13... | collective-permute-start | bytes 1290248 | tf_op jit(solution)/shard_map/ppermute | solution.py:492
  41.0 1.4 %collective-permute-start.18 = (f32[8,128]{1,0:T(8,128)S(1)}, f32[8,128]{1,0:T(8,128)S(1)}, u32[]{:S(2)}, u32[]{:S(2)}) collective-permute-start(f32[8,128]{1,0:T(8,128)S(1)} %get-tuple-element.131.refs_0_), channel_id=1, source_target_pairs={{0,4},{4,0},{8,12},{12,8},{16,20},{20,16},{24,28},{28,24},{1,5},{5... | collective-permute-start | bytes 12296 | tf_op jit(solution)/shard_map/ppermute | solution.py:497
  45.7 3.4 %collective-permute-start.19 = (f32[8,128]{1,0:T(8,128)S(1)}, f32[8,128]{1,0:T(8,128)S(1)}, u32[]{:S(2)}, u32[]{:S(2)}) collective-permute-start(f32[8,128]{1,0:T(8,128)S(1)} %get-tuple-element.132.refs_1_), channel_id=1, source_target_pairs={{0,8},{4,12},{8,0},{12,4},{16,24},{20,28},{24,16},{28,20},{1,9},{5... | collective-permute-start | bytes 12296 | tf_op jit(solution)/shard_map/ppermute | solution.py:497
  49.1 9.7 %collective-permute-start.24 = (f32[264,128]{1,0:T(8,128)S(1)}, f32[264,128]{1,0:T(8,128)S(1)}, u32[]{:S(2)}, u32[]{:S(2)}) collective-permute-start(f32[264,128]{1,0:T(8,128)S(1)} %get-tuple-element.137), channel_id=1, source_target_pairs={{0,1},{1,2},{2,3},{3,0},{4,5},{5,6},{6,7},{7,4},{8,9},{9,10},{10,1... | collective-permute-start | bytes 405512 | tf_op jit(solution)/shard_map/ppermute | solution.py:488
  49.1 12.6 %collective-permute-start.25 = (f32[264,128]{1,0:T(8,128)S(1)}, f32[264,128]{1,0:T(8,128)S(1)}, u32[]{:S(2)}, u32[]{:S(2)}) collective-permute-start(f32[264,128]{1,0:T(8,128)S(1)} %get-tuple-element.138), channel_id=1, source_target_pairs={{0,2},{1,3},{2,0},{3,1},{4,6},{5,7},{6,4},{7,5},{8,10},{9,11},{10,... | collective-permute-start | bytes 405512 | tf_op jit(solution)/shard_map/ppermute | solution.py:488
  50.3 4.9 %collective-permute-start.23 = (f32[8,128]{1,0:T(8,128)S(1)}, f32[8,128]{1,0:T(8,128)S(1)}, u32[]{:S(2)}, u32[]{:S(2)}) collective-permute-start(f32[8,128]{1,0:T(8,128)S(1)} %get-tuple-element.136.refs_1_), channel_id=1, source_target_pairs={{0,16},{4,20},{8,24},{12,28},{16,0},{20,4},{24,8},{28,12},{1,17},{... | collective-permute-start | bytes 12296 | tf_op jit(solution)/shard_map/ppermute | solution.py:497
  51.4 25.9 %collective-permute-start.29 = (f32[904,128]{1,0:T(8,128)S(1)}, f32[904,128]{1,0:T(8,128)S(1)}, u32[]{:S(2)}, u32[]{:S(2)}) collective-permute-start(f32[904,128]{1,0:T(8,128)S(1)} %get-tuple-element.145), channel_id=1, source_target_pairs={{4,0},{8,4},{12,8},{16,12},{20,16},{24,20},{28,24},{5,1},{9,5},{13... | collective-permute-start | bytes 1388552 | tf_op jit(solution)/shard_map/ppermute | solution.py:492
  55.3 22.0 %collective-permute-start.30 = (f32[904,128]{1,0:T(8,128)S(1)}, f32[904,128]{1,0:T(8,128)S(1)}, u32[]{:S(2)}, u32[]{:S(2)}) collective-permute-start(f32[904,128]{1,0:T(8,128)S(1)} %get-tuple-element.146), channel_id=1, source_target_pairs={{0,4},{4,8},{8,12},{12,16},{16,20},{20,24},{24,28},{1,5},{5,9},{9,... | collective-permute-start | bytes 1388552 | tf_op jit(solution)/shard_map/ppermute | solution.py:492
  58.8 15.4 %collective-permute-start.28 = (f32[840,128]{1,0:T(8,128)S(1)}, f32[840,128]{1,0:T(8,128)S(1)}, u32[]{:S(2)}, u32[]{:S(2)}) collective-permute-start(f32[840,128]{1,0:T(8,128)S(1)} %get-tuple-element.142), channel_id=1, source_target_pairs={{0,4},{4,8},{8,12},{12,16},{16,20},{20,24},{24,28},{1,5},{5,9},{9,... | collective-permute-start | bytes 1290248 | tf_op jit(solution)/shard_map/ppermute | solution.py:492
  61.7 6.1 %collective-permute-start.26 = (f32[264,128]{1,0:T(8,128)S(1)}, f32[264,128]{1,0:T(8,128)S(1)}, u32[]{:S(2)}, u32[]{:S(2)}) collective-permute-start(f32[264,128]{1,0:T(8,128)S(1)} %get-tuple-element.139), channel_id=1, source_target_pairs={{0,3},{1,0},{2,1},{3,2},{4,7},{5,4},{6,5},{7,6},{8,11},{9,8},{10,9... | collective-permute-start | bytes 405512 | tf_op jit(solution)/shard_map/ppermute | solution.py:488
  68.6 8.7 %collective-permute-start.31 = (f32[392,128]{1,0:T(8,128)S(1)}, f32[392,128]{1,0:T(8,128)S(1)}, u32[]{:S(2)}, u32[]{:S(2)}) collective-permute-start(f32[392,128]{1,0:T(8,128)S(1)} %get-tuple-element.147), channel_id=1, source_target_pairs={{4,0},{8,4},{12,8},{16,12},{20,16},{24,20},{28,24},{5,1},{9,5},{13... | collective-permute-start | bytes 602120 | tf_op jit(solution)/shard_map/ppermute | solution.py:492
  71.6 5.7 %collective-permute-start.32 = (f32[392,128]{1,0:T(8,128)S(1)}, f32[392,128]{1,0:T(8,128)S(1)}, u32[]{:S(2)}, u32[]{:S(2)}) collective-permute-start(f32[392,128]{1,0:T(8,128)S(1)} %get-tuple-element.148), channel_id=1, source_target_pairs={{0,4},{4,8},{8,12},{12,16},{16,20},{20,24},{24,28},{1,5},{5,9},{9,... | collective-permute-start | bytes 602120 | tf_op jit(solution)/shard_map/ppermute | solution.py:492
